TPU v7x, 128 devices: a whole 4x4x4 slice. The times are simulated.
128 devices in a mesh: dp: 4 (over x), tensor: 32 (over z, y, core).
Axes of the slice: x: 4, y: 4, z: 4, core: 2. Of those that a mesh axis runs over, the one named last changes fastest.
Arguments:
- tokens: bfloat16 [8192, 2048], P(('dp', 'tensor')), may hold values from -40 to 40
- attn_gain: bfloat16 [2048], replicated, may hold values from 0.099609375 to 1.8984375
- moe_gain: bfloat16 [2048], replicated, may hold values from 0.099609375 to 1.8984375
- q_gain: bfloat16 [128], replicated, may hold values from 0.099609375 to 1.8984375
- k_gain: bfloat16 [128], replicated, may hold values from 0.099609375 to 1.8984375
- query_weight: bfloat16 [2048, 4096], P(None, 'tensor'), may hold values from -0.125 to 0.125
- w_kv: bfloat16 [256, 4, 2048], P('tensor'), may hold values from -0.125 to 0.125
- w_o: bfloat16 [4096, 2048], P('tensor'), may hold values from -0.5 to 0.5
- w_gate: bfloat16 [64, 768, 2048], P('tensor'), may hold values from -0.125 to 0.125
- w_up: bfloat16 [64, 768, 2048], P('tensor'), may hold values from -0.125 to 0.125
- w_down: bfloat16 [64, 768, 2048], P('tensor'), may hold values from -0.21875 to 0.21875
- shrink_qkv: bfloat16 [16, 48, 2048], P('dp'), may hold values from -0.125 to 0.125
- shrink_o: bfloat16 [16, 16, 4096], P(None, None, 'tensor'), may hold values from -0.5 to 0.5
- query_up_factors: bfloat16 [16, 16, 4096], P(None, None, 'tensor'), may hold values from -1.5 to 1.5
- key_value_up_factors: bfloat16 [16, 16, 1024], replicated, may hold values from -1.5 to 1.5
- expand_o: bfloat16 [16, 16, 2048], replicated, may hold values from -1.5 to 1.5
- lengths: int32 [4, 32], P('dp'), may hold values from 1 to 256, 2048 in all within a row
- groups: int32 [4, 32], P('dp'), may hold values from 0 to 3, never falling along the last dimension, each value on 1 to 16 neighbouring positions
- adapter_of_request: int32 [4, 32], P('dp'), may hold values from 0 to 15
- adapter_slot: int32 [16], replicated, may hold values from 0 to 15, each once
- page_table: int32 [4, 64], P('dp'), may hold values from 0 to 63, each once within a row
- expert_ids: int32 [8192, 8], P('dp'), may hold values from 0 to 63, all different within a row; in each aligned block of 64 rows (0 to 63, 64 to 127, ...) at most 16 rows name the same one
- expert_gates: float32 [8192, 8], P('dp'), may hold values from 0.05 to 1
Outputs:
- attn_out: bfloat16 [8192, 2048], P(('dp', 'tensor'))
- moe_out: bfloat16 [8192, 2048], P(('dp', 'tensor'))
- kv_pages: bfloat16 [256, 1024, 128], P('dp', 'tensor')
Inputs may be any that keep to these rules, and one draw needn't show every extreme that they name: `lengths`: each row sums to 2048; its largest entry is exactly 256. `groups`: never falling along a row; each group holds 1 to 16 consecutive requests, one exactly 16. `adapter_slot`: A permutation; the factors of slots k * 16 / 4 to (k + 1) * 16 / 4 - 1 are held at dp index k. `page_table`: each row is a permutation of the pages of that token group's pool. `expert_ids`: A token's 8 experts are distinct; within each aligned block of 64 rows (the rows of one device) no expert is chosen by more than 16 tokens, a bound that some block reaches.
All inputs are finite; a program needn't handle non-finite values.
Results may differ from a plain program's by a relative error of at most 0.025.
Values may be sent and summed in bfloat16 or wider, within the bound.
A program may use at most 128 MiB of HBM per device.

v0:
```python
import math
import jax
import jax.numpy as jnp
from jax import lax
from jax.sharding import PartitionSpec as P

EXPERTS = 64
PAGE = 128
CAP_DEV = 16
NORM_EPS = 1e-06
ROPE_BASE = 1000000.0
ADAPTER_FACTOR = 0.5


def normalize(values, gain):
    return (
        values
        * lax.rsqrt(jnp.mean(values * values, axis=-1, keepdims=True) + NORM_EPS)
        * gain.astype(jnp.float32)
    )


def rotate(values, position):
    half = values.shape[-1] // 2
    freq = jnp.exp(
        -jnp.arange(half, dtype=jnp.float32) * (2.0 * math.log(ROPE_BASE) / values.shape[-1])
    )
    angle = position.astype(jnp.float32)[:, None, None] * freq[None, None, :]
    cosine = jnp.cos(angle)
    sine = jnp.sin(angle)
    first = values[..., :half]
    second = values[..., half:]
    return jnp.concatenate(
        [first * cosine - second * sine, second * cosine + first * sine], axis=-1
    )


def lookup(index_value, table):
    match = index_value[:, None] == jnp.arange(table.shape[0], dtype=jnp.int32)[None, :]
    return jnp.sum(jnp.where(match, table[None, :], 0), axis=1)


def token_layout(length_row, group_row, adapter_row, adapter_slot, page_row, grand_total):
    position = jnp.arange(grand_total, dtype=jnp.int32)
    ends = jnp.cumsum(length_row)
    starts = ends - length_row
    request = jnp.sum((ends[None, :] <= position[:, None]).astype(jnp.int32), axis=1)
    group = lookup(request, group_row)
    same = group_row[:, None] == group_row[None, :]
    group_first = jnp.min(jnp.where(same, starts[None, :], grand_total), axis=1)
    rope_pos = position - lookup(request, group_first)
    offset = position - lookup(request, starts)
    per_request = page_row.shape[0] // length_row.shape[0]
    page = lookup(request * per_request + offset // PAGE, page_row)
    cell = page * PAGE + offset % PAGE
    adapter_position = lookup(request, lookup(adapter_row, adapter_slot))
    return (group, rope_pos, cell, adapter_position)


def spread_rows(values, adapter_position, adapters):
    match = adapter_position[:, None] == jnp.arange(adapters, dtype=jnp.int32)[None, :]
    placed = jnp.where(match[:, :, None], values[:, None, :], jnp.zeros((), values.dtype))
    return placed.reshape(values.shape[0], -1)


def attend(query_rows_out, keys, values, group, scale):
    grand_total = query_rows_out.shape[0]
    block = min(512, grand_total)
    position = jnp.arange(grand_total, dtype=jnp.int32)

    def one_block(number):
        first = number * block
        query_block = lax.dynamic_slice_in_dim(query_rows_out, first, block, 0)
        rows_here = first + jnp.arange(block, dtype=jnp.int32)
        group_here = lax.dynamic_slice_in_dim(group, first, block, 0)
        allowed = (position[None, :] <= rows_here[:, None]) & (
            group[None, :] == group_here[:, None]
        )
        scores = (
            jnp.einsum("qhd,kd->hqk", query_block, keys, preferred_element_type=jnp.float32) * scale
        )
        raised = jnp.where(allowed[None], jnp.exp(scores), 0.0)
        shares = (raised / jnp.sum(raised, axis=-1, keepdims=True)).astype(jnp.bfloat16)
        mixed = jnp.einsum("hqk,kd->qhd", shares, values, preferred_element_type=jnp.float32)
        return mixed.astype(jnp.bfloat16).reshape(block, -1)

    return lax.map(one_block, jnp.arange(grand_total // block, dtype=jnp.int32)).reshape(
        grand_total, -1
    )


def expert_apply(rows, gate_rows, up_rows, down_rows):
    gate_value = jnp.einsum("secx,efx->secf", rows, gate_rows, preferred_element_type=jnp.float32)
    up_value = jnp.einsum("secx,efx->secf", rows, up_rows, preferred_element_type=jnp.float32)
    hidden = (jax.nn.silu(gate_value) * up_value).astype(jnp.bfloat16)
    out = jnp.einsum("secf,efx->secx", hidden, down_rows, preferred_element_type=jnp.float32)
    return lax.optimization_barrier(out.astype(jnp.bfloat16))


def local(
    tokens,
    attn_gain,
    moe_gain,
    q_gain,
    k_gain,
    query_weight,
    w_kv,
    w_o,
    w_gate,
    w_up,
    w_down,
    shrink_qkv,
    shrink_o,
    query_up_factors,
    key_value_up_factors,
    expand_o,
    lengths,
    groups,
    adapter_of_request,
    adapter_slot,
    page_table,
    expert_ids,
    expert_gates,
):
    parts = lax.axis_size("tensor")
    place = lax.axis_index("tensor")
    own_rows, width = tokens.shape
    grand_total = own_rows * parts
    head_length = q_gain.shape[0]
    adapters, rank, kv_width = key_value_up_factors.shape
    key_value_heads = kv_width // (2 * head_length)
    group, rope_pos, cell, adapter_position = token_layout(
        lengths[0], groups[0], adapter_of_request[0], adapter_slot, page_table[0], grand_total
    )
    own_slot = lax.dynamic_slice_in_dim(adapter_position, place * own_rows, own_rows, 0)
    normed_own = normalize(tokens.astype(jnp.float32), attn_gain).astype(jnp.bfloat16)
    piece = lax.all_gather(shrink_qkv, "dp", axis=0, tiled=True)
    projected = jnp.einsum("td,prd->tpr", normed_own, piece, preferred_element_type=jnp.float32)
    match = own_slot[:, None] == jnp.arange(piece.shape[0], dtype=jnp.int32)[None, :]
    shrunk_own = jnp.sum(jnp.where(match[:, :, None], projected, 0.0), axis=1)
    shrunk_own = shrunk_own.astype(jnp.bfloat16)
    normalized_input, shrunken_rows = (
        lax.all_gather(normed_own, "tensor", axis=0, tiled=True),
        lax.all_gather(shrunk_own, "tensor", axis=0, tiled=True),
    )
    head = place * key_value_heads // parts
    local_cols = kv_width // parts
    token_extent = w_kv.shape[0]
    span_begin = place * token_extent
    base_key_value = jnp.einsum(
        "td,chd->thc", normalized_input, w_kv, preferred_element_type=jnp.float32
    )
    upward_split = key_value_up_factors.reshape(adapters, rank, key_value_heads, 2 * head_length)
    upward_local = lax.dynamic_slice_in_dim(upward_split, span_begin, token_extent, 3).reshape(
        adapters * rank, key_value_heads * token_extent
    )
    key_adapter_delta = jnp.dot(
        spread_rows(shrunken_rows[:, rank : 2 * rank], adapter_position, adapters),
        upward_local,
        preferred_element_type=jnp.float32,
    )
    value_adapter_delta = jnp.dot(
        spread_rows(shrunken_rows[:, 2 * rank :], adapter_position, adapters),
        upward_local,
        preferred_element_type=jnp.float32,
    )
    whether_key = jnp.tile(
        span_begin + jnp.arange(token_extent, dtype=jnp.int32) < head_length, key_value_heads
    )
    adapter_delta_term = jnp.where(
        whether_key[None, :], key_adapter_delta, value_adapter_delta
    ).reshape(grand_total, key_value_heads, token_extent)
    resident_key_value = (base_key_value + ADAPTER_FACTOR * adapter_delta_term).astype(jnp.bfloat16)
    every_kv = lax.all_gather(resident_key_value, "tensor", axis=2, tiled=True)
    head_kv = lax.dynamic_index_in_dim(every_kv, head, 1, keepdims=False)
    divided_key_value = head_kv.reshape(grand_total, 2, head_length)
    keys = rotate(normalize(divided_key_value[:, :1].astype(jnp.float32), k_gain), rope_pos).astype(
        jnp.bfloat16
    )[:, 0]
    values = divided_key_value[:, 1]
    entries = jnp.concatenate([keys, values], axis=1)
    mine = lax.dynamic_slice_in_dim(
        entries, place * local_cols - head * 2 * head_length, local_cols, 1
    )
    pages_held = page_table.shape[1]
    kv_pages = jnp.zeros((pages_held * PAGE, local_cols), jnp.bfloat16).at[cell].set(mine)
    kv_pages = kv_pages.reshape(pages_held, PAGE, local_cols).transpose(0, 2, 1)
    query_cols = query_weight.shape[1]
    heads_here = query_cols // head_length
    query_rows_out = jnp.dot(
        normalized_input, query_weight, preferred_element_type=jnp.float32
    ) + ADAPTER_FACTOR * jnp.dot(
        spread_rows(shrunken_rows[:, :rank], adapter_position, adapters),
        query_up_factors.reshape(adapters * rank, query_cols),
        preferred_element_type=jnp.float32,
    )
    query_rows_out = rotate(
        normalize(query_rows_out.reshape(grand_total, heads_here, head_length), q_gain), rope_pos
    ).astype(jnp.bfloat16)
    mixed = attend(query_rows_out, keys, values, group, head_length ** (-0.5))
    shrink_table = shrink_o.reshape(adapters * rank, query_cols)
    upward_wide_rows = expand_o.reshape(adapters * rank, width).astype(jnp.float32)
    lower_rank_rows = lax.dot_general(
        mixed, shrink_table, (((1,), (1,)), ((), ())), preferred_element_type=jnp.float32
    )
    retained_mask = jnp.repeat(
        adapter_position[:, None] == jnp.arange(adapters, dtype=jnp.int32)[None, :], rank, axis=1
    )
    adapter_contribution = jnp.dot(mixed, w_o, preferred_element_type=jnp.float32)
    attn_own = lax.psum_scatter(
        (
            adapter_contribution
            + ADAPTER_FACTOR
            * jnp.dot(
                jnp.where(retained_mask, lower_rank_rows, 0.0),
                upward_wide_rows,
                precision=lax.Precision.HIGHEST,
            )
        ).astype(jnp.bfloat16),
        "tensor",
        scatter_dimension=0,
        tiled=True,
    ).astype(jnp.float32)
    moe_own = normalize(tokens.astype(jnp.float32) + attn_own, moe_gain).astype(jnp.bfloat16)
    experts_here = w_gate.shape[0]
    moe_in = lax.all_gather(moe_own, "tensor", axis=0, tiled=True)
    own_experts = place * experts_here + jnp.arange(experts_here, dtype=jnp.int32)
    choose = expert_ids[:, :, None] == own_experts[None, None, :]
    share = expert_gates / jnp.sum(expert_gates, axis=1, keepdims=True)
    weight = jnp.sum(jnp.where(choose, share[:, :, None], 0.0), axis=1)
    hit = jnp.any(choose, axis=1).reshape(parts, own_rows, experts_here)
    weight = weight.reshape(parts, own_rows, experts_here)
    below = jnp.tril(jnp.ones((own_rows, own_rows), jnp.bfloat16))
    rank_in_block = jnp.einsum(
        "ut,ste->sue", below, hit.astype(jnp.bfloat16), preferred_element_type=jnp.float32
    )
    numbers = jnp.arange(1, CAP_DEV + 1, dtype=jnp.float32)
    picked = hit[..., None] & (rank_in_block[..., None] == numbers)
    pick = picked.astype(jnp.bfloat16)
    slot_weight = jnp.sum(jnp.where(picked, weight[..., None], 0.0), axis=1)
    rows = jnp.einsum(
        "stek,std->eskd",
        pick,
        moe_in.reshape(parts, own_rows, width),
        preferred_element_type=jnp.float32,
    ).astype(jnp.bfloat16)
    rows = rows.reshape(1, experts_here, parts * CAP_DEV, width)
    outputs = expert_apply(rows, w_gate, w_up, w_down)[0]
    slot_weight = slot_weight.transpose(1, 0, 2).reshape(experts_here, parts * CAP_DEV, 1)
    weighted = (outputs.astype(jnp.float32) * slot_weight).astype(jnp.bfloat16)
    moe_terms = jnp.einsum(
        "stek,eskd->std",
        pick,
        weighted.reshape(experts_here, parts, CAP_DEV, width),
        preferred_element_type=jnp.float32,
    ).reshape(grand_total, width)
    moe_total = lax.psum_scatter(
        moe_terms.astype(jnp.bfloat16), "tensor", scatter_dimension=0, tiled=True
    )
    return (attn_own.astype(jnp.bfloat16), moe_total, kv_pages)


def solution(mesh):
    placed = (
        P(("dp", "tensor"), None),
        P(),
        P(),
        P(),
        P(),
        P(None, "tensor"),
        P("tensor", None, None),
        P("tensor", None),
        P("tensor", None, None),
        P("tensor", None, None),
        P("tensor", None, None),
        P("dp", None, None),
        P(None, None, "tensor"),
        P(None, None, "tensor"),
        P(),
        P(),
        P("dp", None),
        P("dp", None),
        P("dp", None),
        P(),
        P("dp", None),
        P("dp", None),
        P("dp", None),
    )
    return jax.shard_map(
        local,
        mesh=mesh,
        in_specs=placed,
        out_specs=(P(("dp", "tensor"), None), P(("dp", "tensor"), None), P("dp", "tensor", None)),
        check_vma=False,
    )
```

profile of v0, /device:TPU:0, one launch (start us, length us, event | category | flops | bytes accessed | tf_op | source)
XLA Modules:
  0.0 492.1 jit_solution(7418017794389099014)
XLA Ops:
  12.7 5.8 %copy.123 = bf16[16,16,1024]{1,0,2:T(8,128)(2,1)} copy(bf16[16,16,1024]{2,1,0:T(8,128)(2,1)} %param.39) | data formatting | bytes 1048576 | tf_op jit(solution)/shard_map/reshape | solution.py:153
  20.3 31.4 %all-gather.8.cloned.1.call-done = bf16[16,48,2048]{2,1,0:T(8,128)(2,1)} async-done(((bf16[4,48,2048]{2,1,0:T(8,128)(2,1)}), bf16[16,48,2048]{2,1,0:T(8,128)(2,1)}) %all-gather.8.cloned.1.call-update) | async-done | bytes 3145744 | tf_op jit(solution)/shard_map/all_gather | solution.py:137
  51.7 2.9 fusion.37
  54.6 25.1 %all-gather = bf16[32,64,48]{1,2,0:T(8,128)(2,1)S(1)} all-gather(bf16[1,64,48]{1,2,0:T(8,128)(2,1)S(1)} %bitcast.218), channel_id=1, replica_groups=mesh['dp'=4,'tensor'=32] {'tensor'}, dimensions={0}, use_global_device_ids=true | all-gather | bytes 202752 | tf_op jit(solution)/shard_map/all_gather | solution.py:144
  80.7 27.3 %all-gather.6.cloned.1.call-done = bf16[2048,2048]{1,0:T(8,128)(2,1)} async-done(((bf16[64,2048]{1,0:T(8,128)(2,1)}), bf16[2048,2048]{1,0:T(8,128)(2,1)}) %all-gather.6.cloned.1.call-update) | async-done | bytes 8388624 | tf_op jit(solution)/shard_map/all_gather | solution.py:143
  108.0 5.9 %fusion.28 = f32[2048,4,8]{0,2,1:T(8,128)S(1)} fusion(bf16[2048,2048]{1,0:T(8,128)(2,1)} %all-gather.6.cloned.1.call-done, bf16[8,4,2048]{2,1,0:T(4,128)(2,1)S(1)} %copy-done.22), kind=kOutput, calls=%fused_computation.35 | convolution fusion | flops 268435456 | bytes 8781824 | tf_op jit(solution)/shard_map/td,chd->thc/dot_general | solution.py:150
  116.7 6.3 %fusion.89 = f32[2048,128]{0,1:T(8,128)S(1)} fusion(bf16[2048,2048]{1,0:T(8,128)(2,1)} %all-gather.6.cloned.1.call-done, bf16[2048,128]{1,0:T(8,128)(2,1)S(1)} %copy-done.12), kind=kOutput, calls=%fused_computation.159 | convolution fusion | flops 1073741824 | bytes 9961472 | tf_op jit(solution)/shard_map/dot_general | solution.py:190
  123.7 37.3 %all-gather.10.cloned.1.call-done = bf16[2048,4,256]{0,2,1:T(8,128)(2,1)} async-done(((bf16[2048,4,8]{0,2,1:T(8,128)(2,1)}), bf16[2048,4,256]{0,2,1:T(8,128)(2,1)}) %all-gather.10.cloned.1.call-update) | async-done | bytes 4194320 | tf_op jit(solution)/shard_map/all_gather | solution.py:174
  162.6 3.4 fusion.67
  169.9 19.9 %while.11 = (s32[]{:T(128)}, bf16[4,512,128]{2,1,0:T(8,128)(2,1)S(1)}, s32[4]{0:T(128)S(1)}, s32[2048]{0:T(1024)S(1)}, bf16[2048,1,128]{0,2,1:T(8,128)(2,1)}, /*...) while((s32[]{:T(128)}, ...), condition=%wide.region_13.14_spmd.clone, body=%wide.region_11.13_spmd.clone.sunk | while | flops 545325056 | bytes 11819227 | solution.py:87
  171.3 2.8 fusion.127
  176.2 2.8 fusion.127
  181.2 2.8 fusion.127
  186.2 2.8 fusion.127
  190.6 3.5 fusion.90
  195.9 12.1 %add_convert_fusion = bf16[2048,2048]{1,0:T(8,128)(2,1)} fusion(f32[2048,2048]{1,0:T(8,128)S(1)} %fusion.90, f32[2048,256]{1,0:T(8,128)} %convolution_select_fusion, bf16[256,2048]{1,0:T(8,128)(2,1)S(1)} %bitcast.197), kind=kOutput, calls=%fused_computation.16 | convolution fusion | flops 12897484800 | bytes 28311552 | tf_op jit(solution)/shard_map/dot_general | solution.py:214
  208.7 91.6 %reduce-scatter.3.cloned.1.call-done = bf16[64,2048]{1,0:T(8,128)(2,1)} async-done(((bf16[2048,2048]{1,0:T(8,128)(2,1)}), bf16[64,2048]{1,0:T(8,128)(2,1)}) %reduce-scatter.3.cloned.1.call-update) | async-done | bytes 262160 | tf_op jit(solution)/shard_map/reduce_scatter | solution.py:210
  305.0 50.6 %all-gather.12.cloned.1.call-done = bf16[2048,2048]{1,0:T(8,128)(2,1)} async-done(((bf16[64,2048]{1,0:T(8,128)(2,1)}), bf16[2048,2048]{1,0:T(8,128)(2,1)}) %all-gather.12.cloned.1.call-update) | async-done | bytes 8388624 | tf_op jit(solution)/shard_map/all_gather | solution.py:226
  355.6 4.6 fusion.91
  363.4 7.9 %fusion.92 = f32[2,512,768]{2,1,0:T(8,128)} fusion(bf16[2,512,2048]{2,1,0:T(8,128)(2,1)S(1)} %bitcast.208, bf16[2,768,2048]{2,1,0:T(8,128)(2,1)} %param.34), kind=kOutput, calls=%fused_computation.162 | convolution fusion | flops 3221225472 | bytes 13631488 | tf_op jit(solution)/shard_map/secx,efx->secf/dot_general | solution.py:94
  371.3 13.4 %convert_bitcast_fusion = bf16[1,2,512,2048]{3,2,1,0:T(8,128)(2,1)} fusion(bf16[2,768,2048]{2,1,0:T(8,128)(2,1)} %param.35, f32[2,512,768]{2,1,0:T(8,128)} %fusion.92, bf16[2,512,2048]{2,1,0:T(8,128)(2,1)} %bitcast.209, bf16[2,768,2048]{2,1,0:T(8,128)(2,1)} %param.33), kind=kOutput, calls=%fused_computation.22 | convolution fusion | flops 6449266688 | bytes 24117248 | tf_op jit(solution)/shard_map/secf,efx->secx/dot_general | solution.py:96
  384.7 7.9 %bitcast_convert_fusion = bf16[32,64,2048]{2,1,0:T(8,128)(2,1)} fusion(f32[2,32,16]{2,0,1:T(2,128)S(1)} %bitcast.215, f32[32,64,2]{1,2,0:T(2,128)S(1)} %copy.115, f32[16]{0:T(128)S(1)} %iota_add_fusion.1, pred[32,64,2]{1,2,0:T(4,128)(4,1)S(1)} %copy.114, bf16[2,32,16,2048]{3,2,1,0:T(8,128)(2,1)} %bitcast.206), kind=kOutput, calls=%fused_computation.15 | convolution fusion | flops 279052288 | bytes 12607552 | tf_op jit(solution)/shard_map/stek,eskd->std/dot_general | solution.py:251
  394.7 6.8 %scatter_custom_fusion = bf16[8192,32]{1,0:T(8,128)(2,1)S(1)} fusion(s32[2048]{0:T(1024)S(1)} %bitcast.220, bf16[2048,32]{1,0:T(8,128)(2,1)} %copy.119, bf16[]{:T(256)} %constant.56.clone.1), kind=kCustom, calls=%fused_computation.53 | custom fusion | bytes 524800 | tf_op jit(solution)/shard_map/scatter | solution.py:186
  403.1 82.0 %reduce-scatter.5.cloned.1.call-done = bf16[64,2048]{1,0:T(8,128)(2,1)} async-done(((bf16[2048,2048]{1,0:T(8,128)(2,1)}), bf16[64,2048]{1,0:T(8,128)(2,1)}) %reduce-scatter.5.cloned.1.call-update) | async-done | bytes 262160 | tf_op jit(solution)/shard_map/reduce_scatter | solution.py:257
  (163 shorter events, 37.8 us)
Async XLA Ops:
  7.2 188.8 %copy-start = (bf16[16,16,2048]{2,1,0:T(8,128)(2,1)S(1)}, bf16[16,16,2048]{2,1,0:T(8,128)(2,1)}, u32[]{:S(2)}) copy-start(bf16[16,16,2048]{2,1,0:T(8,128)(2,1)} %param.40) | copy-start | bytes 3145732
  7.2 12.5 %copy-start.20 = (s32[1,32]{1,0:T(1,128)S(1)}, s32[1,32]{1,0:T(1,128)}, u32[]{:S(2)}) copy-start(s32[1,32]{1,0:T(1,128)} %param.41) | copy-start | bytes 388
  7.2 12.3 %copy-start.24 = (s32[16]{0:T(128)S(1)}, s32[16]{0:T(128)}, u32[]{:S(2)}) copy-start(s32[16]{0:T(128)} %param.44) | copy-start | bytes 196
  7.2 12.3 %copy-start.25 = (s32[1,32]{1,0:T(1,128)S(1)}, s32[1,32]{1,0:T(1,128)}, u32[]{:S(2)}) copy-start(s32[1,32]{1,0:T(1,128)} %param.43) | copy-start | bytes 388
  7.2 12.4 %copy-start.18 = (s32[1,32]{1,0:T(1,128)S(1)}, s32[1,32]{1,0:T(1,128)}, u32[]{:S(2)}) copy-start(s32[1,32]{1,0:T(1,128)} %param.42) | copy-start | bytes 388
  7.2 44.5 %all-gather.8.cloned.1.call-start = ((), (), s32[]{:S(2)}) async-start(), calls=%async_computation.3 | async-start | bytes 3932160 | tf_op jit(solution)/shard_map/all_gather | solution.py:137
  8.0 100.0 %all-gather.6.cloned.1.call-start = ((), (), s32[]{:S(2)}) async-start(), calls=%async_computation.2 | async-start | bytes 8650752 | tf_op jit(solution)/shard_map/all_gather | solution.py:143
  11.6 40.1 %copy-start.6 = (bf16[64,2048]{1,0:T(8,128)(2,1)S(1)}, bf16[64,2048]{1,0:T(8,128)(2,1)}, u32[]{:S(2)}) copy-start(bf16[64,2048]{1,0:T(8,128)(2,1)} %fusion.62) | copy-start | bytes 786436
  11.6 149.3 %all-gather.10.cloned.1.call-start = ((), (), s32[]{:S(2)}) async-start(), calls=%async_computation.4 | async-start | bytes 4325376 | tf_op jit(solution)/shard_map/all_gather | solution.py:174
  20.3 87.7 %copy-start.22 = (bf16[8,4,2048]{2,1,0:T(4,128)(2,1)S(1)}, bf16[8,4,2048]{2,1,0:T(4,128)(2,1)}, u32[]{:S(2)}) copy-start(bf16[8,4,2048]{2,1,0:T(4,128)(2,1)} %param.31) | copy-start | bytes 393220
  80.7 34.3 %copy-start.26 = (bf16[128]{0:T(256)(128)(2,1)S(1)}, bf16[128]{0:T(256)(128)(2,1)}, u32[]{:S(2)}) copy-start(bf16[128]{0:T(256)(128)(2,1)} %param.28) | copy-start | bytes 772
  80.7 34.3 %copy-start.27 = (bf16[128]{0:T(256)(128)(2,1)S(1)}, bf16[128]{0:T(256)(128)(2,1)}, u32[]{:S(2)}) copy-start(bf16[128]{0:T(256)(128)(2,1)} %param.29) | copy-start | bytes 772
  80.7 36.0 %copy-start.12 = (bf16[2048,128]{1,0:T(8,128)(2,1)S(1)}, bf16[2048,128]{1,0:T(8,128)(2,1)}, u32[]{:S(2)}) copy-start(bf16[2048,128]{1,0:T(8,128)(2,1)} %param.30) | copy-start | bytes 1572868
  114.9 185.3 %reduce-scatter.3.cloned.1.call-start = ((), (), s32[]{:S(2)}) async-start(), calls=%async_computation.5 | async-start | bytes 8650752 | tf_op jit(solution)/shard_map/reduce_scatter | solution.py:210
  116.7 6.3 %copy-start.23 = (bf16[16,16,128]{2,1,0:T(8,128)(2,1)S(1)}, bf16[16,16,128]{2,1,0:T(8,128)(2,1)}, u32[]{:S(2)}) copy-start(bf16[16,16,128]{2,1,0:T(8,128)(2,1)} %param.38) | copy-start | bytes 196612
  166.0 3.9 copy-start.7
  169.9 20.7 %copy-start.13 = (bf16[128,2048]{1,0:T(8,128)(2,1)S(1)}, bf16[128,2048]{1,0:T(8,128)(2,1)}, u32[]{:S(2)}) copy-start(bf16[128,2048]{1,0:T(8,128)(2,1)} %param.32) | copy-start | bytes 1572868
  190.6 3.5 copy-start.17
  208.0 92.2 %copy-start.3 = (bf16[64,2048]{1,0:T(8,128)(2,1)S(1)}, bf16[64,2048]{1,0:T(8,128)(2,1)}, u32[]{:S(2)}) copy-start(bf16[64,2048]{1,0:T(8,128)(2,1)} %param.25) | copy-start | bytes 786436
  208.0 95.7 %copy-start.16 = (s32[2048,8]{0,1:T(8,128)S(1)}, s32[2048,8]{0,1:T(8,128)}, u32[]{:S(2)}) copy-start(s32[2048,8]{0,1:T(8,128)} %param.46) | copy-start | bytes 196612
  208.0 96.2 %copy-start.15 = (f32[2048,8]{0,1:T(8,128)S(1)}, f32[2048,8]{0,1:T(8,128)}, u32[]{:S(2)}) copy-start(f32[2048,8]{0,1:T(8,128)} %param.47) | copy-start | bytes 196612
  208.0 147.6 %all-gather.12.cloned.1.call-start = ((), (), s32[]{:S(2)}) async-start(), calls=%async_computation.6 | async-start | bytes 8650752 | tf_op jit(solution)/shard_map/all_gather | solution.py:226
  303.2 181.9 %reduce-scatter.5.cloned.1.call-start = ((), (), s32[]{:S(2)}) async-start(), calls=%async_computation.7 | async-start | bytes 8650752 | tf_op jit(solution)/shard_map/reduce_scatter | solution.py:257
  392.6 92.5 %copy-start.1 = (bf16[16,16,2048]{2,1,0:T(8,128)(2,1)S(1)}, bf16[16,16,2048]{2,1,0:T(8,128)(2,1)}, u32[]{:S(2)}) copy-start(bf16[16,16,2048]{2,1,0:T(8,128)(2,1)} %param.40) | copy-start | bytes 3145732
  (13 other events, 25.3 us)
Sparse Core Ops, SparseCore 0:
  9.7 41.9 all-gather.7
  54.6 53.3 all-gather.5
  115.0 45.9 all-gather.9
  208.1 92.0 reduce-scatter.2
  303.3 52.2 all-gather.11
  392.7 92.3 reduce-scatter.4
where the time goes:
time: 501 us; the launch traced here: 492 us
  waiting for transfers between devices  321 us (64%)
  matrix products  82.3 us (16%)
  local copies, waits for them, and re-layouts  30.3 us (6%)
  blocking collectives  25.1 us (5%)
  other arithmetic  15.1 us (3%)
  between operations  14.9 us (3%)
    reduce_scatter x1, waiting for transfers between devices, local(): lax.psum_scatter((adapter_contribution + ADAPTER_FACTOR * jnp.dot(jnp.whe...  91.6 us
    reduce_scatter x1, waiting for transfers between devices, local(): lax.psum_scatter(moe_terms.astype(jnp.bfloat16), 'tensor', scatter_dimens...  82 us
    all_gather x1, waiting for transfers between devices, local(): moe_in = lax.all_gather(moe_own, 'tensor', axis=0, tiled=True)  50.6 us
    all_gather x1, waiting for transfers between devices, local(): every_kv = lax.all_gather(resident_key_value, 'tensor', axis=2, tiled=True)  37.3 us
    all_gather x1, waiting for transfers between devices, local(): piece = lax.all_gather(shrink_qkv, 'dp', axis=0, tiled=True)  31.4 us
    all_gather x1, waiting for transfers between devices, local(): lax.all_gather(normed_own, 'tensor', axis=0, tiled=True)  27.3 us
    all_gather x1, blocking collectives, local(): lax.all_gather(shrunk_own, 'tensor', axis=0, tiled=True)  25.1 us
    dot_general x1, matrix products, expert_apply(): jnp.einsum('secf,efx->secx', hidden, down_rows, preferred_element_type=jn...  13.4 us
  transfers between devices with their start and end apart: 6, of which 6 were waited for; matrix products, arithmetic and copies ran while one was open for 7% of the time, Pallas kernels for 0%

commit v1 on v0

--- a/solution.py
+++ b/solution.py
@@ -10,6 +10,27 @@
 NORM_EPS = 1e-06
 ROPE_BASE = 1000000.0
 ADAPTER_FACTOR = 0.5
+
+
+def collect(x, axis, dim):
+    count, index, width = (lax.axis_size(axis), lax.axis_index(axis), x.shape[dim])
+    right = [(i, (i + 1) % count) for i in range(count)]
+    left = [(i, (i - 1) % count) for i in range(count)]
+    out = jnp.zeros((*x.shape[:dim], count * width, *x.shape[dim + 1 :]), x.dtype)
+    out = lax.dynamic_update_slice_in_dim(out, x, index * width, axis=dim)
+    from_left = from_right = x
+    halfway = count // 2
+    for hop in range(1, halfway + 1):
+        from_left = lax.ppermute(from_left, axis, right)
+        out = lax.dynamic_update_slice_in_dim(
+            out, from_left, (index - hop) % count * width, axis=dim
+        )
+        if hop < count - halfway:
+            from_right = lax.ppermute(from_right, axis, left)
+            out = lax.dynamic_update_slice_in_dim(
+                out, from_right, (index + hop) % count * width, axis=dim
+            )
+    return out
 
 
 def normalize(values, gain):
@@ -134,7 +155,7 @@
     )
     own_slot = lax.dynamic_slice_in_dim(adapter_position, place * own_rows, own_rows, 0)
     normed_own = normalize(tokens.astype(jnp.float32), attn_gain).astype(jnp.bfloat16)
-    piece = lax.all_gather(shrink_qkv, "dp", axis=0, tiled=True)
+    piece = collect(shrink_qkv, "dp", 0)
     projected = jnp.einsum("td,prd->tpr", normed_own, piece, preferred_element_type=jnp.float32)
     match = own_slot[:, None] == jnp.arange(piece.shape[0], dtype=jnp.int32)[None, :]
     shrunk_own = jnp.sum(jnp.where(match[:, :, None], projected, 0.0), axis=1)

time: 501 us -> 470 us (0.938)
  waiting for transfers between devices: 321 us -> 285 us
    all_gather x1 -> x0, waiting for transfers between devices: 31.4 us -> none  [local(): piece = lax.all_gather(shrink_qkv, 'dp', axis=0, tiled=True)]
    all_gather x1, waiting for transfers between devices: 27.3 us -> 0.02 us  [local(): lax.all_gather(normed_own, 'tensor', axis=0, tiled=True)]
    ppermute x0 -> x3, waiting for transfers between devices: none -> 26 us  [the longest x2 26 us: collect(): from_left = lax.ppermute(from_left, axis, right)]
  transfers between devices with their start and end apart: 6 -> 8, of which waited for: 6 -> 6; matrix products, arithmetic and copies ran while one was open for 7% -> 7% of each run, Pallas kernels for 0% -> 0%
where the time goes in v1:
time: 470 us; the launch traced here: 462 us
  waiting for transfers between devices  285 us (61%)
  matrix products  80.5 us (17%)
  local copies, waits for them, and re-layouts  33.4 us (7%)
  blocking collectives  26.6 us (6%)
  other arithmetic  14.9 us (3%)
  between operations  14.6 us (3%)
    reduce_scatter x1, waiting for transfers between devices, local(): lax.psum_scatter((adapter_contribution + ADAPTER_FACTOR * jnp.dot(jnp.whe...  91.6 us
    reduce_scatter x1, waiting for transfers between devices, local(): lax.psum_scatter(moe_terms.astype(jnp.bfloat16), 'tensor', scatter_dimens...  82.1 us
    all_gather x1, waiting for transfers between devices, local(): moe_in = lax.all_gather(moe_own, 'tensor', axis=0, tiled=True)  50.9 us
    all_gather x1, waiting for transfers between devices, local(): every_kv = lax.all_gather(resident_key_value, 'tensor', axis=2, tiled=True)  34.3 us
    all_gather x1, blocking collectives, local(): lax.all_gather(shrunk_own, 'tensor', axis=0, tiled=True)  26.6 us
    ppermute x2, waiting for transfers between devices, collect(): from_left = lax.ppermute(from_left, axis, right)  26 us
    dot_general x1, matrix products, expert_apply(): jnp.einsum('secf,efx->secx', hidden, down_rows, preferred_element_type=jn...  13.5 us
    dot_general x1, matrix products, local(): jnp.dot(jnp.where(retained_mask, lower_rank_rows, 0.0), upward_wide_rows,...  12.1 us
  transfers between devices with their start and end apart: 8, of which 6 were waited for; matrix products, arithmetic and copies ran while one was open for 7% of the time, Pallas kernels for 0%

profile of v1, /device:TPU:0, one launch (start us, length us, event | category | flops | bytes accessed | tf_op | source)
XLA Modules:
  0.0 462.5 jit_solution(2820196397781115830)
XLA Ops:
  15.2 5.8 %copy.123 = bf16[16,16,1024]{1,0,2:T(8,128)(2,1)} copy(bf16[16,16,1024]{2,1,0:T(8,128)(2,1)} %param.39) | data formatting | bytes 1048576 | tf_op jit(solution)/shard_map/reshape | solution.py:174
  22.8 8.9 %collective-permute-done = bf16[4,48,2048]{2,1,0:T(8,128)(2,1)S(1)} collective-permute-done((bf16[4,48,2048]{2,1,0:T(8,128)(2,1)}, bf16[4,48,2048]{2,1,0:T(8,128)(2,1)S(1)}, u32[]{:S(2)}, u32[]{:S(2)}) %collective-permute-start) | collective-permute-done | bytes 786464 | tf_op jit(solution)/shard_map/ppermute | solution.py:24
  34.2 17.1 %collective-permute-done.2 = bf16[4,48,2048]{2,1,0:T(8,128)(2,1)} collective-permute-done((bf16[4,48,2048]{2,1,0:T(8,128)(2,1)S(1)}, bf16[4,48,2048]{2,1,0:T(8,128)(2,1)}, u32[]{:S(2)}, u32[]{:S(2)}) %collective-permute-start.2) | collective-permute-done | bytes 786464 | tf_op jit(solution)/shard_map/ppermute | solution.py:24
  53.6 26.6 %all-gather = bf16[32,64,48]{1,2,0:T(8,128)(2,1)S(1)} all-gather(bf16[1,64,48]{1,2,0:T(8,128)(2,1)S(1)} %bitcast.217), channel_id=1, replica_groups=mesh['dp'=4,'tensor'=32] {'tensor'}, dimensions={0}, use_global_device_ids=true | all-gather | bytes 202752 | tf_op jit(solution)/shard_map/all_gather | solution.py:165
  81.2 5.9 %fusion.28 = f32[2048,4,8]{0,2,1:T(8,128)S(1)} fusion(bf16[2048,2048]{1,0:T(8,128)(2,1)} %all-gather.5.cloned.1.call-done, bf16[8,4,2048]{2,1,0:T(4,128)(2,1)S(1)} %copy-done.23), kind=kOutput, calls=%fused_computation.35 | convolution fusion | flops 268435456 | bytes 8781824 | tf_op jit(solution)/shard_map/td,chd->thc/dot_general | solution.py:171
  90.5 6.3 %fusion.89 = f32[2048,128]{0,1:T(8,128)S(1)} fusion(bf16[2048,2048]{1,0:T(8,128)(2,1)} %all-gather.5.cloned.1.call-done, bf16[2048,128]{1,0:T(8,128)(2,1)S(1)} %copy-done.13), kind=kOutput, calls=%fused_computation.163 | convolution fusion | flops 1073741824 | bytes 9961472 | tf_op jit(solution)/shard_map/dot_general | solution.py:211
  97.4 34.3 %all-gather.7.cloned.1.call-done = bf16[2048,4,256]{0,2,1:T(8,128)(2,1)} async-done(((bf16[2048,4,8]{0,2,1:T(8,128)(2,1)}), bf16[2048,4,256]{0,2,1:T(8,128)(2,1)}) %all-gather.7.cloned.1.call-update) | async-done | bytes 4194320 | tf_op jit(solution)/shard_map/all_gather | solution.py:195
  133.4 3.1 fusion.67
  140.5 19.8 %while.11 = (s32[]{:T(128)}, bf16[4,512,128]{2,1,0:T(8,128)(2,1)S(1)}, s32[4]{0:T(128)S(1)}, s32[2048]{0:T(1024)S(1)}, bf16[2048,1,128]{0,2,1:T(8,128)(2,1)}, /*...) while((s32[]{:T(128)}, ...), condition=%wide.region_13.14_spmd.clone, body=%wide.region_11.13_spmd.clone.sunk | while | flops 545325056 | bytes 11819219 | solution.py:108
  141.8 2.8 fusion.127
  146.7 2.8 fusion.127
  151.7 2.8 fusion.127
  156.7 2.8 fusion.127
  161.1 3.5 fusion.90
  166.4 12.1 %add_convert_fusion = bf16[2048,2048]{1,0:T(8,128)(2,1)} fusion(f32[2048,2048]{1,0:T(8,128)S(1)} %fusion.90, f32[2048,256]{1,0:T(8,128)} %convolution_select_fusion, bf16[256,2048]{1,0:T(8,128)(2,1)S(1)} %bitcast.196), kind=kOutput, calls=%fused_computation.16 | convolution fusion | flops 12897484800 | bytes 28311552 | tf_op jit(solution)/shard_map/dot_general | solution.py:235
  179.1 91.6 %reduce-scatter.3.cloned.1.call-done = bf16[64,2048]{1,0:T(8,128)(2,1)} async-done(((bf16[2048,2048]{1,0:T(8,128)(2,1)}), bf16[64,2048]{1,0:T(8,128)(2,1)}) %reduce-scatter.3.cloned.1.call-update) | async-done | bytes 262160 | tf_op jit(solution)/shard_map/reduce_scatter | solution.py:231
  275.2 50.9 %all-gather.9.cloned.1.call-done = bf16[2048,2048]{1,0:T(8,128)(2,1)} async-done(((bf16[64,2048]{1,0:T(8,128)(2,1)}), bf16[2048,2048]{1,0:T(8,128)(2,1)}) %all-gather.9.cloned.1.call-update) | async-done | bytes 8388624 | tf_op jit(solution)/shard_map/all_gather | solution.py:247
  326.1 4.6 fusion.91
  332.0 1.9 copy-done.2
  333.9 7.9 %fusion.92 = f32[2,512,768]{2,1,0:T(8,128)} fusion(bf16[2,512,2048]{2,1,0:T(8,128)(2,1)S(1)} %bitcast.207, bf16[2,768,2048]{2,1,0:T(8,128)(2,1)} %param.34), kind=kOutput, calls=%fused_computation.166 | convolution fusion | flops 3221225472 | bytes 13631488 | tf_op jit(solution)/shard_map/secx,efx->secf/dot_general | solution.py:115
  341.8 13.5 %convert_bitcast_fusion = bf16[1,2,512,2048]{3,2,1,0:T(8,128)(2,1)} fusion(bf16[2,768,2048]{2,1,0:T(8,128)(2,1)} %param.35, f32[2,512,768]{2,1,0:T(8,128)} %fusion.92, bf16[2,512,2048]{2,1,0:T(8,128)(2,1)} %bitcast.208, bf16[2,768,2048]{2,1,0:T(8,128)(2,1)} %param.33), kind=kOutput, calls=%fused_computation.22 | convolution fusion | flops 6449266688 | bytes 24117248 | tf_op jit(solution)/shard_map/secf,efx->secx/dot_general | solution.py:117
  355.3 7.9 %bitcast_convert_fusion = bf16[32,64,2048]{2,1,0:T(8,128)(2,1)} fusion(f32[2,32,16]{2,0,1:T(2,128)S(1)} %bitcast.214, f32[32,64,2]{1,2,0:T(2,128)S(1)} %copy.115, f32[16]{0:T(128)S(1)} %iota_add_fusion.1, pred[32,64,2]{1,2,0:T(4,128)(4,1)S(1)} %copy.114, bf16[2,32,16,2048]{3,2,1,0:T(8,128)(2,1)} %bitcast.205), kind=kOutput, calls=%fused_computation.15 | convolution fusion | flops 279052288 | bytes 12607552 | tf_op jit(solution)/shard_map/stek,eskd->std/dot_general | solution.py:272
  365.3 6.8 %scatter_custom_fusion = bf16[8192,32]{1,0:T(8,128)(2,1)S(1)} fusion(s32[2048]{0:T(1024)S(1)} %bitcast.219, bf16[2048,32]{1,0:T(8,128)(2,1)} %copy.119, bf16[]{:T(256)} %constant.123.clone.1), kind=kCustom, calls=%fused_computation.53 | custom fusion | bytes 524800 | tf_op jit(solution)/shard_map/scatter | solution.py:207
  373.6 82.1 %reduce-scatter.5.cloned.1.call-done = bf16[64,2048]{1,0:T(8,128)(2,1)} async-done(((bf16[2048,2048]{1,0:T(8,128)(2,1)}), bf16[64,2048]{1,0:T(8,128)(2,1)}) %reduce-scatter.5.cloned.1.call-update) | async-done | bytes 262160 | tf_op jit(solution)/shard_map/reduce_scatter | solution.py:278
  (173 shorter events, 43.2 us)
Async XLA Ops:
  7.2 159.2 %copy-start = (bf16[16,16,2048]{2,1,0:T(8,128)(2,1)S(1)}, bf16[16,16,2048]{2,1,0:T(8,128)(2,1)}, u32[]{:S(2)}) copy-start(bf16[16,16,2048]{2,1,0:T(8,128)(2,1)} %param.40) | copy-start | bytes 3145732
  7.2 14.0 %copy-start.21 = (s32[1,32]{1,0:T(1,128)S(1)}, s32[1,32]{1,0:T(1,128)}, u32[]{:S(2)}) copy-start(s32[1,32]{1,0:T(1,128)} %param.41) | copy-start | bytes 388
  7.2 13.9 %copy-start.26 = (s32[1,32]{1,0:T(1,128)S(1)}, s32[1,32]{1,0:T(1,128)}, u32[]{:S(2)}) copy-start(s32[1,32]{1,0:T(1,128)} %param.43) | copy-start | bytes 388
  7.2 13.9 %copy-start.25 = (s32[16]{0:T(128)S(1)}, s32[16]{0:T(128)}, u32[]{:S(2)}) copy-start(s32[16]{0:T(128)} %param.44) | copy-start | bytes 196
  7.2 14.0 %copy-start.19 = (s32[1,32]{1,0:T(1,128)S(1)}, s32[1,32]{1,0:T(1,128)}, u32[]{:S(2)}) copy-start(s32[1,32]{1,0:T(1,128)} %param.42) | copy-start | bytes 388
  7.2 74.0 %all-gather.5.cloned.1.call-start = ((), (), s32[]{:S(2)}) async-start(), calls=%async_computation.2 | async-start | bytes 8650752 | tf_op jit(solution)/shard_map/all_gather | solution.py:164
  11.0 120.8 %all-gather.7.cloned.1.call-start = ((), (), s32[]{:S(2)}) async-start(), calls=%async_computation.3 | async-start | bytes 4325376 | tf_op jit(solution)/shard_map/all_gather | solution.py:195
  11.0 20.7 %collective-permute-start = (bf16[4,48,2048]{2,1,0:T(8,128)(2,1)}, bf16[4,48,2048]{2,1,0:T(8,128)(2,1)S(1)}, u32[]{:S(2)}, u32[]{:S(2)}) collective-permute-start(bf16[4,48,2048]{2,1,0:T(8,128)(2,1)} %param.36), channel_id=1, source_target_pairs={{0,32},{32,64},{64,96},{96,0},{1,33},{33,65},{65,97},{97,1},{2,34}... | collective-permute-start | bytes 2359304 | tf_op jit(solution)/shard_map/ppermute | solution.py:24
  12.7 20.3 %collective-permute-start.1 = (bf16[4,48,2048]{2,1,0:T(8,128)(2,1)}, bf16[4,48,2048]{2,1,0:T(8,128)(2,1)}, u32[]{:S(2)}, u32[]{:S(2)}) collective-permute-start(bf16[4,48,2048]{2,1,0:T(8,128)(2,1)} %param.36), channel_id=1, source_target_pairs={{0,96},{32,0},{64,32},{96,64},{1,97},{33,1},{65,33},{97,65},{2,98}... | collective-permute-start | bytes 2359304 | tf_op jit(solution)/shard_map/ppermute | solution.py:29
  15.2 17.6 %copy-start.12 = (bf16[4,48,2048]{2,1,0:T(8,128)(2,1)S(1)}, bf16[4,48,2048]{2,1,0:T(8,128)(2,1)}, u32[]{:S(2)}) copy-start(bf16[4,48,2048]{2,1,0:T(8,128)(2,1)} %param.36) | copy-start | bytes 2359300
  31.7 19.6 %collective-permute-start.2 = (bf16[4,48,2048]{2,1,0:T(8,128)(2,1)S(1)}, bf16[4,48,2048]{2,1,0:T(8,128)(2,1)}, u32[]{:S(2)}, u32[]{:S(2)}) collective-permute-start(bf16[4,48,2048]{2,1,0:T(8,128)(2,1)S(1)} %collective-permute-done), channel_id=1, source_target_pairs={{0,32},{32,64},{64,96},{96,0},{1,33},{33,65},{65,97},{97,1},{2,34}... | collective-permute-start | bytes 2359304 | tf_op jit(solution)/shard_map/ppermute | solution.py:24
  32.4 20.2 %copy-start.6 = (bf16[64,2048]{1,0:T(8,128)(2,1)S(1)}, bf16[64,2048]{1,0:T(8,128)(2,1)}, u32[]{:S(2)}) copy-start(bf16[64,2048]{1,0:T(8,128)(2,1)} %fusion.62) | copy-start | bytes 786436
  52.6 28.6 %copy-start.23 = (bf16[8,4,2048]{2,1,0:T(4,128)(2,1)S(1)}, bf16[8,4,2048]{2,1,0:T(4,128)(2,1)}, u32[]{:S(2)}) copy-start(bf16[8,4,2048]{2,1,0:T(4,128)(2,1)} %param.31) | copy-start | bytes 393220
  81.2 7.5 %copy-start.27 = (bf16[128]{0:T(256)(128)(2,1)S(1)}, bf16[128]{0:T(256)(128)(2,1)}, u32[]{:S(2)}) copy-start(bf16[128]{0:T(256)(128)(2,1)} %param.28) | copy-start | bytes 772
  81.2 7.6 %copy-start.28 = (bf16[128]{0:T(256)(128)(2,1)S(1)}, bf16[128]{0:T(256)(128)(2,1)}, u32[]{:S(2)}) copy-start(bf16[128]{0:T(256)(128)(2,1)} %param.29) | copy-start | bytes 772
  81.2 9.3 %copy-start.13 = (bf16[2048,128]{1,0:T(8,128)(2,1)S(1)}, bf16[2048,128]{1,0:T(8,128)(2,1)}, u32[]{:S(2)}) copy-start(bf16[2048,128]{1,0:T(8,128)(2,1)} %param.30) | copy-start | bytes 1572868
  88.2 182.6 %reduce-scatter.3.cloned.1.call-start = ((), (), s32[]{:S(2)}) async-start(), calls=%async_computation.4 | async-start | bytes 8650752 | tf_op jit(solution)/shard_map/reduce_scatter | solution.py:231
  140.4 20.6 %copy-start.14 = (bf16[128,2048]{1,0:T(8,128)(2,1)S(1)}, bf16[128,2048]{1,0:T(8,128)(2,1)}, u32[]{:S(2)}) copy-start(bf16[128,2048]{1,0:T(8,128)(2,1)} %param.32) | copy-start | bytes 1572868
  178.5 92.3 %copy-start.3 = (bf16[64,2048]{1,0:T(8,128)(2,1)S(1)}, bf16[64,2048]{1,0:T(8,128)(2,1)}, u32[]{:S(2)}) copy-start(bf16[64,2048]{1,0:T(8,128)(2,1)} %param.25) | copy-start | bytes 786436
  178.5 95.5 %copy-start.17 = (s32[2048,8]{0,1:T(8,128)S(1)}, s32[2048,8]{0,1:T(8,128)}, u32[]{:S(2)}) copy-start(s32[2048,8]{0,1:T(8,128)} %param.46) | copy-start | bytes 196612
  178.5 95.9 %copy-start.16 = (f32[2048,8]{0,1:T(8,128)S(1)}, f32[2048,8]{0,1:T(8,128)}, u32[]{:S(2)}) copy-start(f32[2048,8]{0,1:T(8,128)} %param.47) | copy-start | bytes 196612
  178.5 147.6 %all-gather.9.cloned.1.call-start = ((), (), s32[]{:S(2)}) async-start(), calls=%async_computation.5 | async-start | bytes 8650752 | tf_op jit(solution)/shard_map/all_gather | solution.py:247
  273.7 182.0 %reduce-scatter.5.cloned.1.call-start = ((), (), s32[]{:S(2)}) async-start(), calls=%async_computation.6 | async-start | bytes 8650752 | tf_op jit(solution)/shard_map/reduce_scatter | solution.py:278
  363.2 92.5 %copy-start.1 = (bf16[16,16,2048]{2,1,0:T(8,128)(2,1)S(1)}, bf16[16,16,2048]{2,1,0:T(8,128)(2,1)}, u32[]{:S(2)}) copy-start(bf16[16,16,2048]{2,1,0:T(8,128)(2,1)} %param.40) | copy-start | bytes 3145732
  (16 other events, 39.0 us)
Sparse Core Ops, SparseCore 0:
  11.1 55.6 all-gather.4
  88.3 43.4 all-gather.6
  178.6 92.0 reduce-scatter.2
  273.8 52.2 all-gather.8
  363.3 92.3 reduce-scatter.4
